TPU v7x, 32 devices: a whole 2x2x4 slice. The times are simulated.
32 devices in a mesh: row: 8 (over z, core), col: 4 (over y, x).
Axes of the slice: x: 2, y: 2, z: 4, core: 2. Of those that a mesh axis runs over, the one named last changes fastest.
Arguments:
- features: bfloat16 [9, 1, 128, 128, 128], P(None, None, 'row', 'col'), may hold values from -12 to 12
- cotangent: float32 [3, 1, 128, 128, 128], P(None, None, 'row', 'col'), may hold values from -14 to 14
- w_in: bfloat16 [9, 256], replicated, may hold values from -2 to 2
- bias_in: float32 [256], replicated, may hold values from -3 to 3
- w_mid: bfloat16 [256, 256], replicated, may hold values from -0.375 to 0.375
- bias_mid: float32 [256], replicated, may hold values from -3 to 3
- w_out: bfloat16 [256, 6], replicated, may hold values from -2.5 to 2.5
Outputs:
- grad_features: float32 [9, 1, 128, 128, 128], P(None, None, 'row', 'col')
- grad_w_in: float32 [9, 256], replicated
- grad_b_in: float32 [256], replicated
- grad_w_mid: float32 [256, 256], replicated
- grad_b_mid: float32 [256], replicated
- grad_w_out: float32 [256, 6], replicated
All inputs are finite; a program needn't handle non-finite values.
Results may differ from a plain program's by a relative error of at most 0.025.
Values sent between devices are 32-bit elements; how exact they have to be, the bound alone decides.
A program may use at most 128 MiB of HBM per device.

v0:
```python
import math

import jax
import jax.numpy as jnp
from jax import lax
from jax.sharding import PartitionSpec as P

NX = 128
NY = 128
NZ = 128
CELLS = 2097152


STEP_DT = 0.04
PAIRS = ((0, 0), (1, 1), (2, 2), (0, 1), (0, 2), (1, 2))


def mode_list(count, length):
    index = jnp.arange(count, dtype=jnp.int32)
    return jnp.where(index < length // 2, index, index - length)


def phase_table(modes, length):
    positions = jnp.arange(length, dtype=jnp.int32)
    turns = positions[:, None] * modes[None, :] % length
    angle = turns.astype(jnp.float32) * (2.0 * math.pi / length)
    return (jnp.cos(angle), jnp.sin(angle))


def contract(form, left, right):
    return jnp.einsum(
        form, left, right, precision=lax.Precision.HIGHEST, preferred_element_type=jnp.float32
    )


def complex_product(form, part, table_real, table_imag):
    real = contract(form, part[0], table_real) - contract(form, part[1], table_imag)
    imag = contract(form, part[0], table_imag) + contract(form, part[1], table_real)
    return jnp.stack([real, imag])


def closure_block(x_blk, g_blk, w_in, bias_in, w_mid, bias_mid, w_out):
    pre_in = (
        jnp.einsum("fh,fn->hn", w_in, x_blk, preferred_element_type=jnp.float32) + bias_in[:, None]
    )
    act_in = jnp.tanh(pre_in).astype(jnp.bfloat16)
    pre_mid = (
        jnp.einsum("io,in->on", w_mid, act_in, preferred_element_type=jnp.float32)
        + bias_mid[:, None]
    )
    act_mid = jnp.tanh(pre_mid).astype(jnp.bfloat16)
    back_mid = jnp.einsum("ho,on->hn", w_out, g_blk, preferred_element_type=jnp.float32)
    delta_mid = (back_mid * (1.0 - jnp.square(act_mid.astype(jnp.float32)))).astype(jnp.bfloat16)
    back_in = jnp.einsum("io,on->in", w_mid, delta_mid, preferred_element_type=jnp.float32)
    delta_in = (back_in * (1.0 - jnp.square(act_in.astype(jnp.float32)))).astype(jnp.bfloat16)
    grad_x = jnp.einsum("fh,hn->fn", w_in, delta_in, preferred_element_type=jnp.float32)
    gw_out = jnp.einsum("hn,on->ho", act_mid, g_blk, preferred_element_type=jnp.float32)
    gw_mid = jnp.einsum("in,on->io", act_in, delta_mid, preferred_element_type=jnp.float32)
    gw_in = jnp.einsum("fn,hn->fh", x_blk, delta_in, preferred_element_type=jnp.float32)
    gb_mid = jnp.sum(delta_mid.astype(jnp.float32), axis=1)
    gb_in = jnp.sum(delta_in.astype(jnp.float32), axis=1)
    return (grad_x, (gw_in, gb_in, gw_mid, gb_mid, gw_out))


def per_device(features, cotangent, w_in, bias_in, w_mid, bias_mid, w_out):
    rows_group = lax.axis_size("row")
    cols_group = lax.axis_size("col")
    count_y = NY
    count_z = NZ
    list_z = mode_list(count_z, NZ)
    weight_z = jnp.ones((count_z,), jnp.float32) / NZ
    list_x = mode_list(NX, NX)
    list_y = mode_list(count_y, NY)
    cos_x, sin_x = phase_table(list_x, NX)
    cos_y, sin_y = phase_table(list_y, NY)
    cos_z, sin_z = phase_table(list_z, NZ)
    forward_z = jnp.stack(
        [
            contract("csxyz,zk->csxky", cotangent, cos_z),
            -contract("csxyz,zk->csxky", cotangent, sin_z),
        ]
    )
    spectra = complex_product(
        "csxky,yq->cskqx",
        lax.all_to_all(forward_z, "col", split_axis=4, concat_axis=5, tiled=True),
        cos_y,
        -sin_y,
    )
    spectra = complex_product(
        "cskqx,xp->cskqp",
        lax.all_to_all(spectra, "row", split_axis=4, concat_axis=5, tiled=True),
        cos_x,
        -sin_x,
    )
    share_y = count_y // rows_group
    share_z = count_z // cols_group
    local_y = lax.dynamic_slice_in_dim(list_y, lax.axis_index("row") * share_y, share_y)
    local_z = lax.dynamic_slice_in_dim(list_z, lax.axis_index("col") * share_z, share_z)
    modes_x = list_x[None, None, :]
    modes_y = local_y[None, :, None]
    modes_z = local_z[:, None, None]
    keep = (3 * jnp.abs(modes_x) < NX) & (3 * jnp.abs(modes_y) < NY) & (3 * jnp.abs(modes_z) < NZ)
    waves = [modes_x.astype(jnp.float32), modes_y.astype(jnp.float32), modes_z.astype(jnp.float32)]
    velocity = [spectra[:, comp] for comp in range(3)]
    inner = waves[0] * velocity[0] + waves[1] * velocity[1] + waves[2] * velocity[2]
    square = jnp.maximum(waves[0] * waves[0] + waves[1] * waves[1] + waves[2] * waves[2], 1.0)
    projected = [
        jnp.where(keep, velocity[comp] - waves[comp] * inner / square, 0.0) for comp in range(3)
    ]
    stress_parts = []
    for first, second in PAIRS:
        if first == second:
            value = waves[first] * projected[first]
        else:
            value = waves[second] * projected[first] + waves[first] * projected[second]
        stress_parts.append(jnp.stack([-STEP_DT * value[1], STEP_DT * value[0]]))
    stress_hat = jnp.stack(stress_parts, axis=1)
    back_x = complex_product("cskqp,px->cskxq", stress_hat, cos_x.T / NX, sin_x.T / NX)
    stress_mid = complex_product(
        "cskxq,qy->csxyk",
        lax.all_to_all(back_x, "row", split_axis=4, concat_axis=5, tiled=True),
        cos_y.T / NY,
        sin_y.T / NY,
    )
    real_z = cos_z.T * weight_z[:, None]
    imag_z = sin_z.T * weight_z[:, None]
    part = lax.all_to_all(stress_mid, "col", split_axis=4, concat_axis=5, tiled=True)
    stress = contract("csxyk,kz->csxyz", part[0], real_z) - contract(
        "csxyk,kz->csxyz", part[1], imag_z
    )
    inputs_count = features.shape[0]
    stress_count = stress.shape[0]
    cells = stress.shape[1] * stress.shape[2] * stress.shape[3] * stress.shape[4]
    feats = features.reshape(inputs_count, cells)
    grads = stress.astype(jnp.bfloat16).reshape(stress_count, cells)
    hidden = w_mid.shape[0]
    blank = jnp.zeros((inputs_count, cells), jnp.float32)
    block = math.gcd(cells, max(1024, cells // 8))

    def visit(index, carry):
        current, totals = carry
        start = (0 + index * block).astype(jnp.int32)
        x_blk = lax.dynamic_slice_in_dim(feats, start, block, 1)
        g_blk = lax.dynamic_slice_in_dim(grads, start, block, 1)
        grad_x, parts = closure_block(x_blk, g_blk, w_in, bias_in, w_mid, bias_mid, w_out)
        current = lax.dynamic_update_slice_in_dim(current, grad_x, start, 1)
        return (current, tuple((a + b for a, b in zip(totals, parts))))

    init = (
        jnp.zeros((inputs_count, hidden), jnp.float32),
        jnp.zeros((hidden,), jnp.float32),
        jnp.zeros((hidden, hidden), jnp.float32),
        jnp.zeros((hidden,), jnp.float32),
        jnp.zeros((hidden, stress_count), jnp.float32),
    )
    field, local = lax.fori_loop(0, cells // block, visit, (blank, init))
    totals = lax.psum((local[0], local[1], local[2], local[3], local[4]), ("row", "col"))
    factor = 1.0 / math.sqrt(CELLS)
    return (
        field.reshape(features.shape),
        totals[0] * factor,
        totals[1] * factor,
        totals[2] * factor,
        totals[3] * factor,
        totals[4] * factor,
    )


def solution(mesh):
    return jax.shard_map(
        per_device,
        mesh=mesh,
        in_specs=(
            P(None, None, "row", "col", None),
            P(None, None, "row", "col", None),
            P(),
            P(),
            P(),
            P(),
            P(),
        ),
        out_specs=(P(None, None, "row", "col", None), P(), P(), P(), P(), P()),
        check_vma=False,
    )
```

profile of v0, /device:TPU:25, one launch (start us, length us, event | category | flops | bytes accessed | tf_op | source)
XLA Modules:
  0.0 851.5 jit_solution(18035341283685795229)
XLA Ops:
  10.6 6.0 copy.51
  16.6 5.9 reshape.562
  22.5 22.2 %all_to_all.60 = f32[4,1,98304]{2,1,0:T(1,128)S(1)} all-to-all(f32[4,1,98304]{2,1,0:T(1,128)} %reshape.562), channel_id=1, replica_groups=mesh['row'=8,'col'=4] {'col'}, dimensions={0} | all-to-all | bytes 3145728 | tf_op jit(solution)/shard_map/all_to_all | solution.py:85
  45.2 6.4 reduce.2
  51.6 6.3 reshape.563
  57.8 6.8 copy.95
  78.0 6.0 copy.53
  83.9 7.6 reshape.564
  91.6 7.3 all-to-all-start.1
  99.6 34.1 %all-to-all-done.1 = f32[8,1,49152]{2,1,0:T(1,128)S(1)} async-done(((f32[8,1,49152]{2,1,0:T(1,128)}), f32[8,1,49152]{2,1,0:T(1,128)S(1)}, u32[]{:S(2)}, u32[]{:S(2)}) %all-to-all-start.1) | async-done | bytes 1572896 | tf_op jit(solution)/shard_map/all_to_all | solution.py:91
  133.7 6.2 reduce.3
  139.9 6.1 reshape.565
  150.6 5.1 fusion.55
  155.6 5.3 fusion.48
  161.4 5.1 fusion.21
  166.5 5.1 fusion.20
  182.4 11.4 %copy.63 = f32[2,6,1,32,128,16]{3,5,1,2,0,4:T(8,128)} copy(f32[2,6,1,32,128,16]{4,3,5,1,2,0:T(8,128)} %pad_maximum_fusion) | data formatting | bytes 6291456 | tf_op jit(solution)/shard_map/stack | solution.py:39
  193.8 10.6 %reshape.566 = f32[8,1,98304]{2,1,0:T(1,128)} reshape(f32[128,2,1,6,16,32]{5,4,3,2,1,0:T(8,128)} %bitcast.283) | data formatting | bytes 6291456
  204.5 76.0 %all_to_all.61 = f32[8,1,98304]{2,1,0:T(1,128)} all-to-all(f32[8,1,98304]{2,1,0:T(1,128)} %reshape.566), channel_id=1, replica_groups=mesh['row'=8,'col'=4] {'row'}, dimensions={0} | all-to-all | bytes 6291456 | tf_op jit(solution)/shard_map/all_to_all | solution.py:121
  280.4 11.7 %reduce.4 = f32[8,98304]{1,0:T(8,128)} reduce(f32[8,1,98304]{2,1,0:T(1,128)} %all_to_all.61, f32[]{:T(128)} %broadcast.808), dimensions={1}, to_apply=%all_to_all.50.reduce_sub_computation | reduce | bytes 6291460 | tf_op jit(solution)/shard_map/all_to_all | solution.py:121
  292.1 10.6 %reshape.567 = f32[128,2,1,6,16,32]{5,4,3,2,1,0:T(8,128)} reshape(f32[8,98304]{1,0:T(8,128)} %reduce.4) | data formatting | bytes 6291456
  302.8 10.4 %copy.64 = f32[2,6,1,32,128,16]{3,5,4,1,0,2:T(8,128)} copy(f32[2,6,1,32,128,16]{3,5,1,2,0,4:T(8,128)} %bitcast.281) | data formatting | bytes 6291456 | tf_op jit(solution)/shard_map/all_to_all | solution.py:121
  313.2 10.7 %fusion.205 = (f32[1,6,1,32,16,8,16]{3,6,4,5,1,0,2:T(8,128)}, f32[1,6,1,32,16,8,16]{3,6,4,5,1,0,2:T(8,128)}) fusion(f32[2,6,1,32,16,8,16]{3,6,4,5,1,0,2:T(8,128)} %bitcast.279), kind=kLoop, calls=%fused_computation.273 | loop fusion | bytes 6291456 | tf_op jit(solution)/shard_map/slice | solution.py:37
  327.6 10.1 %fusion.64 = f32[128,6,32,16]{0,2,3,1:T(8,128)S(1)} fusion(f32[6,32,16,128]{1,3,2,0:T(8,128)S(1)} %bitcast.277, s32[128]{0:T(128)S(1)} %compare_select_fusion), kind=kOutput, calls=%fused_computation.138 | convolution fusion | flops 604225536 | bytes 3146240 | tf_op jit(solution)/shard_map/cskxq,qy->csxyk/dot_general | solution.py:31
  337.7 10.5 %fusion.43 = f32[128,6,32,16]{0,2,3,1:T(8,128)S(1)} fusion(f32[6,32,16,128]{1,3,2,0:T(8,128)S(1)} %bitcast.278, s32[128]{0:T(128)S(1)} %compare_select_fusion), kind=kOutput, calls=%fused_computation.117 | convolution fusion | flops 604225536 | bytes 3146240 | tf_op jit(solution)/shard_map/cskxq,qy->csxyk/dot_general | solution.py:31
  349.1 10.3 %subtract_bitcast_fusion = f32[1,6,1,16,128,32]{4,5,3,1,2,0:T(8,128)S(1)} fusion(f32[128,6,32,16]{0,2,3,1:T(8,128)S(1)} %fusion.64, f32[6,32,16,128]{1,3,2,0:T(8,128)S(1)} %bitcast.275, s32[128]{0:T(128)S(1)} %compare_select_fusion), kind=kOutput, calls=%fused_computation.41 | convolution fusion | flops 604618752 | bytes 4719104 | tf_op jit(solution)/shard_map/cskxq,qy->csxyk/dot_general | solution.py:31
  359.4 10.1 %add_bitcast_fusion = f32[1,6,1,16,128,32]{4,5,3,1,2,0:T(8,128)S(1)} fusion(f32[128,6,32,16]{0,2,3,1:T(8,128)S(1)} %fusion.43, f32[6,32,16,128]{1,3,2,0:T(8,128)S(1)} %bitcast.276, s32[128]{0:T(128)S(1)} %compare_select_fusion), kind=kOutput, calls=%fused_computation.40 | convolution fusion | flops 604618752 | bytes 4719104 | tf_op jit(solution)/shard_map/cskxq,qy->csxyk/dot_general | solution.py:31
  371.5 11.4 %copy.71 = f32[2,6,1,16,128,32]{5,3,1,2,0,4:T(8,128)} copy(f32[2,6,1,16,128,32]{4,5,3,1,2,0:T(8,128)} %pad_maximum_fusion.1) | data formatting | bytes 6291456 | tf_op jit(solution)/shard_map/stack | solution.py:39
  382.9 9.3 %reshape.568 = f32[4,1,196608]{2,1,0:T(1,128)} reshape(f32[128,2,1,6,16,32]{5,4,3,2,1,0:T(8,128)} %bitcast.284) | data formatting | bytes 6291456
  392.2 4.8 all-to-all-start.3
  400.0 32.8 %all-to-all-done.3 = f32[4,1,196608]{2,1,0:T(1,128)} async-done(((f32[4,1,196608]{2,1,0:T(1,128)}), f32[4,1,196608]{2,1,0:T(1,128)}, u32[]{:S(2)}, u32[]{:S(2)}) %all-to-all-start.3) | async-done | bytes 3145760 | tf_op jit(solution)/shard_map/all_to_all | solution.py:127
  432.8 11.9 %reduce.5 = f32[4,196608]{1,0:T(4,128)} reduce(f32[4,1,196608]{2,1,0:T(1,128)} %all-to-all-done.3, f32[]{:T(128)} %broadcast.808), dimensions={1}, to_apply=%all_to_all.53.reduce_sub_computation | reduce | bytes 6291460 | tf_op jit(solution)/shard_map/all_to_all | solution.py:127
  444.7 10.7 %reshape.569 = f32[128,2,1,6,16,32]{5,4,3,2,1,0:T(8,128)} reshape(f32[4,196608]{1,0:T(4,128)} %reduce.5) | data formatting | bytes 6291456
  455.4 16.4 %copy.94 = f32[2,6,1,16,4,32,32]{6,4,5,3,1,2,0:T(4,128)} copy(f32[2,6,1,16,4,32,32]{6,3,1,0,5,4,2:T(8,128)} %bitcast.282) | data formatting | bytes 6291456 | tf_op jit(solution)/shard_map/all_to_all | solution.py:127
  471.9 14.3 %fusion.204 = (f32[1,6,1,16,32,4,32]{6,5,4,3,1,2,0:T(4,128)}, f32[1,6,1,16,32,4,32]{6,5,4,3,1,2,0:T(4,128)}) fusion(f32[2,6,1,16,32,4,32]{6,5,4,3,1,2,0:T(4,128)} %bitcast.280), kind=kLoop, calls=%fused_computation.272 | loop fusion | bytes 6291456 | tf_op jit(solution)/shard_map/slice | solution.py:129
  486.2 6.2 reshape.552
  495.5 5.8 reshape.553
  507.2 165.7 %while.24 = (s32[]{:T(128)}, f32[9,65536]{1,0:T(8,128)}, f32[9,256]{1,0:T(8,128)S(1)}, f32[256]{0:T(256)S(1)}, f32[256,256]{1,0:T(8,128)S(1)}, /*index=5*/f32[25...) while((s32[]{:T(128)}, f32[9,65536]{1,0:T(8,128)}, ...), condition=%wide.region_3.4_spmd.clone, body=%wide.region_0.3_spmd.clone.sunk | while | flops 3422691328 | bytes 157343136 | solution.py:156
  517.1 4.3 fusion.269
  537.8 4.4 fusion.269
  558.5 4.4 fusion.269
  579.2 4.3 fusion.269
  599.9 4.4 fusion.269
  620.6 4.4 fusion.269
  641.3 4.3 fusion.269
  661.9 4.3 fusion.269
  672.9 37.4 %all-reduce = (f32[9,256]{1,0:T(8,128)S(1)}, f32[256]{0:T(256)S(1)}, f32[256]{0:T(256)S(1)}, f32[256,6]{0,1:T(8,128)S(1)}) all-reduce(f32[9,256]{1,0:T(8,128)S(1)} %get-tuple-element.241, f32[256]{0:T(256)S(1)} %get-tuple-element.242, f32[256]{0:T(256)S(1)} %get-tuple-element.244, ...), channel_id=1, replica_groups=mesh['row'=8,'col'=4] {'row','col'}, use_global_device_ids=true, to_apply=%region_4.5 | all-reduce | flops 4352 | bytes 34816 | tf_op jit(solution)/shard_map/psum | solution.py:157
  717.4 125.4 %all-reduce.3.cloned.1.call-done = f32[256,256]{1,0:T(8,128)} async-done(((f32[256,256]{1,0:T(8,128)}), f32[256,256]{1,0:T(8,128)}) %all-reduce.3.cloned.1.call-update) | async-done | bytes 262160 | tf_op jit(solution)/shard_map/psum | solution.py:157
  (252 shorter events, 190.7 us)
Async XLA Ops:
  91.6 42.1 %all-to-all-start.1 = ((f32[8,1,49152]{2,1,0:T(1,128)}), f32[8,1,49152]{2,1,0:T(1,128)S(1)}, u32[]{:S(2)}, u32[]{:S(2)}) async-start(f32[8,1,49152]{2,1,0:T(1,128)} %reshape.564), calls=%async_computation.1 | async-start | bytes 3145728 | tf_op jit(solution)/shard_map/all_to_all | solution.py:91
  327.6 20.5 %slice-start = ((s8[6291456]{0:T(1024)(128)(4,1)}), s8[4194304]{0:T(1024)(128)(4,1)S(1)}, s32[]{:S(2)}) async-start(s8[6291456]{0:T(1024)(128)(4,1)} %bitcast.291), calls=%async_computation.5 | async-start | bytes 8388608
  337.7 10.5 %slice-start.1 = ((s8[6291456]{0:T(1024)(128)(4,1)}), s8[2097152]{0:T(1024)(128)(4,1)S(1)}, s32[]{:S(2)}) async-start(s8[6291456]{0:T(1024)(128)(4,1)} %bitcast.291), calls=%async_computation.6 | async-start | bytes 4194304
  392.2 4.9 copy-start.9
  392.2 40.6 %all-to-all-start.3 = ((f32[4,1,196608]{2,1,0:T(1,128)}), f32[4,1,196608]{2,1,0:T(1,128)}, u32[]{:S(2)}, u32[]{:S(2)}) async-start(f32[4,1,196608]{2,1,0:T(1,128)} %reshape.568), calls=%async_computation.3 | async-start | bytes 6291456 | tf_op jit(solution)/shard_map/all_to_all | solution.py:127
  397.0 445.8 %all-reduce.3.cloned.1.call-start = ((), (), s32[]{:S(2)}) async-start(), calls=%async_computation.4 | async-start | bytes 524288 | tf_op jit(solution)/shard_map/psum | solution.py:157
  504.4 2.8 copy-start.10
  504.4 2.8 copy-start.11
  504.4 2.8 copy-start.12
  504.4 2.8 copy-start.13
  504.4 2.8 copy-start.14
  509.8 3.4 copy-start.3
  513.1 4.0 copy-start.5
  517.1 4.4 copy-start.4
  521.5 3.7 copy-start.2
  525.2 2.3 copy-start.7
  530.5 3.4 copy-start.3
  533.8 4.0 copy-start.5
  537.8 4.4 copy-start.4
  542.2 3.7 copy-start.2
  545.9 2.3 copy-start.7
  551.2 3.4 copy-start.3
  554.5 4.0 copy-start.5
  558.5 4.4 copy-start.4
  562.9 3.7 copy-start.2
  566.6 2.3 copy-start.7
  571.9 3.4 copy-start.3
  575.2 4.0 copy-start.5
  579.2 4.4 copy-start.4
  583.5 3.7 copy-start.2
  592.5 3.4 copy-start.3
  595.9 4.0 copy-start.5
  599.9 4.4 copy-start.4
  604.2 3.7 copy-start.2
  613.3 3.4 copy-start.3
  616.6 4.0 copy-start.5
  620.6 4.4 copy-start.4
  624.9 3.7 copy-start.2
  634.0 3.3 copy-start.3
  637.3 4.0 copy-start.5
  641.3 4.4 copy-start.4
  645.6 3.7 copy-start.2
  654.6 3.4 copy-start.3
  658.0 4.0 copy-start.5
  661.9 4.3 copy-start.4
  666.3 3.7 copy-start.2
  672.9 42.3 %copy-start.8 = (f32[256,256]{1,0:T(8,128)}, f32[256,256]{1,0:T(8,128)S(1)}, u32[]{:S(2)}) copy-start(f32[256,256]{1,0:T(8,128)S(1)} %get-tuple-element.243) | copy-start | bytes 786436
  712.1 132.3 %copy-start.1 = (f32[3,1,16,32,128]{4,3,2,1,0:T(8,128)S(1)}, f32[3,1,16,32,128]{4,3,2,1,0:T(8,128)}, u32[]{:S(2)}) copy-start(f32[3,1,16,32,128]{4,3,2,1,0:T(8,128)} %param.10) | copy-start | bytes 2359300
  (14 other events, 29.0 us)
Sparse Core Ops, SparseCore 0:
  716.9 125.7 all-reduce.2
where the time goes:
time: 862 us; the launch traced here: 851 us
  matrix products  241 us (28%)
  local copies, waits for them, and re-layouts  207 us (24%)
  waiting for transfers between devices  192 us (22%)
  blocking collectives  136 us (16%)
  other arithmetic  46.9 us (5%)
  between operations  14.8 us (2%)
  starting transfers between devices  12.1 us (1%)
    psum x1, waiting for transfers between devices, per_device(): lax.psum((local[0], local[1], local[2], local[3], local[4]), ('row', 'col'))  125 us
    dot_general x20, matrix products, contract(): jnp.einsum(form, left, right, precision=lax.Precision.HIGHEST, preferred_...  80.9 us
    unnamed x35, local copies, waits for them, and re-layouts  76.5 us
    all_to_all x1, blocking collectives, per_device(): lax.all_to_all(back_x, 'row', split_axis=4, concat_axis=5, tiled=True)  76 us
    psum x1, blocking collectives, per_device(): lax.psum((local[0], local[1], local[2], local[3], local[4]), ('row', 'col'))  37.4 us
    dot_general x8, matrix products, closure_block(): jnp.einsum('fh,hn->fn', w_in, delta_in, preferred_element_type=jnp.float32)  34.8 us
    all_to_all x1, waiting for transfers between devices, per_device(): lax.all_to_all(spectra, 'row', split_axis=4, concat_axis=5, tiled=True)  34.1 us
    all_to_all x1, waiting for transfers between devices, per_device(): lax.all_to_all(stress_mid, 'col', split_axis=4, concat_axis=5, tiled=True)  32.8 us
  transfers between devices with their start and end apart: 3, of which 3 were waited for; matrix products, arithmetic and copies ran while one was open for 0% of the time, Pallas kernels for 0%

commit v1 on v0

v1 whole, which is shorter than its diff:
```python
import functools
import math

import jax
import jax.numpy as jnp
import numpy as np
from jax import lax
from jax.experimental import pallas as pl
from jax.experimental.pallas import tpu as pltpu
from jax.sharding import PartitionSpec as P

STEP_DT = 0.04
MESH = pl.DeviceIdType.MESH
HIGHEST = lax.Precision.HIGHEST


def kept_modes(length):
    top = (length - 1) // 3
    return top


def padded(values, parts):
    share = -(-len(values) // parts)
    out = np.zeros((parts * share,), np.int64)
    out[: len(values)] = values
    live = np.zeros((parts * share,), np.float64)
    live[: len(values)] = 1.0
    return out.reshape(parts, share), live.reshape(parts, share)


def angles(modes, length):
    pos = np.arange(length)
    turns = (modes[..., None] * pos) % length
    return turns * (2.0 * math.pi / length)


def forward_complex(modes, live, length):
    a = angles(modes, length)
    c, s = np.cos(a) * live[..., None], np.sin(a) * live[..., None]
    return np.stack([np.stack([c, s], -2), np.stack([-s, c], -2)], -3)


def inverse_complex(modes, live, length):
    a = angles(modes, length)
    c, s = np.cos(a) * live[..., None] / length, np.sin(a) * live[..., None] / length
    return np.stack([np.stack([c, -s], -2), np.stack([s, c], -2)], -3)


def contract_last(left, right):
    return lax.dot_general(
        left, right, (((1,), (1,)), ((), ())), precision=HIGHEST, preferred_element_type=jnp.float32
    )


def f32(a):
    return jnp.asarray(np.ascontiguousarray(a), jnp.float32)


def spectral(cotangent, rows, cols):
    nc, _, bx, by, nz = cotangent.shape
    nx, ny = bx * rows, by * cols
    mz, live_z = padded(np.arange(kept_modes(nz) + 1), cols)
    top_y = kept_modes(ny)
    my, live_y = padded(np.arange(-top_y, top_y + 1), rows)
    top_x = kept_modes(nx)
    mx = np.arange(-top_x, top_x + 1)
    kz, ky, kx = mz.shape[1], my.shape[1], len(mx)
    az = angles(mz, nz)
    table = np.stack([np.cos(az), -np.sin(az)], 1) * live_z[:, None, :, None]
    part = contract_last(f32(table.reshape(cols * 2 * kz, nz)), cotangent.reshape(nc * bx * by, nz))
    part = lax.all_to_all(part.reshape(cols, 2 * kz, nc * bx * by), "col", 0, 0)
    part = part.reshape(cols, 2, kz, nc, bx, by).transpose(2, 3, 4, 1, 0, 5)
    part = part.reshape(kz * nc * bx, 2 * ny)
    table = forward_complex(my, live_y, ny)
    table = table.transpose(0, 2, 1, 3, 4).reshape(rows * 2 * ky, 2 * ny)
    part = contract_last(f32(table), part)
    part = lax.all_to_all(part.reshape(rows, 2 * ky, kz * nc * bx), "row", 0, 0)
    part = part.reshape(rows, 2, ky, kz, nc, bx).transpose(4, 2, 3, 1, 0, 5)
    part = part.reshape(nc * ky * kz, 2 * nx)
    table = forward_complex(mx, np.ones(kx), nx)
    table = table.transpose(1, 0, 2, 3).reshape(2 * kx, 2 * nx)
    hat = contract_last(f32(table), part).reshape(2, kx, nc, ky * kz)
    wave_x = f32(mx)[:, None]
    wave_y = lax.dynamic_index_in_dim(f32(my), lax.axis_index("row"), 0, False)
    wave_z = lax.dynamic_index_in_dim(f32(mz), lax.axis_index("col"), 0, False)
    wave_y = jnp.broadcast_to(wave_y[:, None], (ky, kz)).reshape(1, ky * kz)
    wave_z = jnp.broadcast_to(wave_z[None, :], (ky, kz)).reshape(1, ky * kz)
    waves = [wave_x, wave_y, wave_z]
    vel = [hat[:, :, comp] for comp in range(3)]
    inner = waves[0] * vel[0] + waves[1] * vel[1] + waves[2] * vel[2]
    square = jnp.maximum(waves[0] * waves[0] + waves[1] * waves[1] + waves[2] * waves[2], 1.0)
    keep = (
        (3 * jnp.abs(waves[0]) < nx) & (3 * jnp.abs(waves[1]) < ny) & (3 * jnp.abs(waves[2]) < nz)
    )
    proj = [jnp.where(keep, vel[i] - waves[i] * inner / square, 0.0) for i in range(3)]
    sent = []
    for a, b in ((1, 1), (2, 2), (0, 1), (0, 2), (1, 2)):
        value = waves[a] * proj[a] if a == b else waves[b] * proj[a] + waves[a] * proj[b]
        sent.append(STEP_DT * value)
    ns = len(sent)
    part = jnp.stack(sent, axis=2).reshape(2 * kx, ns * ky * kz)
    table = inverse_complex(mx, np.ones(kx), nx)
    table = np.stack([table[:, :, 1], -table[:, :, 0]], 2)
    table = table.reshape(kx, 2, 2, rows, bx).transpose(3, 1, 4, 2, 0).reshape(rows * 2 * bx, 2 * kx)
    part = jnp.dot(f32(table), part, precision=HIGHEST, preferred_element_type=jnp.float32)
    part = lax.all_to_all(part.reshape(rows, 2 * bx, ns * ky * kz), "row", 0, 0)
    part = part.reshape(rows, 2, bx, ns, ky, kz).transpose(2, 3, 5, 1, 0, 4)
    part = part.reshape(bx * ns * kz, 2 * rows * ky)
    table = inverse_complex(my, live_y, ny)
    table = table.reshape(rows, ky, 2, 2, cols, by).transpose(4, 2, 5, 3, 0, 1)
    part = contract_last(f32(table.reshape(cols * 2 * by, 2 * rows * ky)), part)
    part = lax.all_to_all(part.reshape(cols, 2 * by, bx * ns * kz), "col", 0, 0)
    part = part.reshape(cols, 2, by, bx, ns, kz).transpose(4, 3, 2, 1, 0, 5)
    part = part.reshape(ns * bx * by, 2 * cols * kz)
    weight = np.where(mz == 0, 1.0, 2.0) * live_z / nz
    table = np.stack([np.cos(az), -np.sin(az)], 0) * weight[None, :, :, None]
    part = jnp.dot(
        part,
        f32(table.reshape(2 * cols * kz, nz)),
        precision=HIGHEST,
        preferred_element_type=jnp.float32,
    ).reshape(ns, bx * by * nz)
    return jnp.concatenate([-(part[0:1] + part[1:2]), part], axis=0)


def closure_kernel(steps, feat, s_ref, w1_ref, b1_ref, w2t_ref, w2_ref, b2_ref, wo_ref, wi_ref,
                   gx_ref, out_ref, left, accm, acci, acco):
    step = pl.program_id(0)
    hid = w2_ref.shape[0]
    ext = s_ref.shape[0]
    trans = (((1,), (1,)), ((), ()))

    @pl.when(step == 0)
    def _():
        accm[...] = jnp.zeros_like(accm)
        acci[...] = jnp.zeros_like(acci)
        acco[...] = jnp.zeros_like(acco)

    s = s_ref[...]
    left[pl.ds(hid, ext), :] = s
    pre = jnp.dot(w1_ref[...], s, preferred_element_type=jnp.float32) + b1_ref[...]
    act_in = jnp.tanh(pre).astype(jnp.bfloat16)
    left[pl.ds(0, hid), :] = act_in
    pre = jnp.dot(w2t_ref[...], act_in, preferred_element_type=jnp.float32) + b2_ref[...]
    act_mid = jnp.tanh(pre).astype(jnp.bfloat16)
    wide = act_mid.astype(jnp.float32)
    back = jnp.dot(wo_ref[...], s, preferred_element_type=jnp.float32)
    delta_mid = (back * (1.0 - wide * wide)).astype(jnp.bfloat16)
    acco[...] += lax.dot_general(s, act_mid, trans, preferred_element_type=jnp.float32)
    accm[...] += lax.dot_general(left[...], delta_mid, trans, preferred_element_type=jnp.float32)
    back = jnp.dot(w2_ref[...], delta_mid, preferred_element_type=jnp.float32)
    wide = left[pl.ds(0, hid), :].astype(jnp.float32)
    delta_in = (back * (1.0 - wide * wide)).astype(jnp.bfloat16)
    acci[...] += lax.dot_general(s, delta_in, trans, preferred_element_type=jnp.float32)
    grad = jnp.dot(wi_ref[...], delta_in, preferred_element_type=jnp.float32)
    gx_ref[...] = grad[:feat]

    @pl.when(step == steps - 1)
    def _():
        out_ref[...] = jnp.zeros_like(out_ref)
        out_ref[pl.ds(0, hid), :] = accm[pl.ds(0, hid), :]
        out_ref[pl.ds(hid, ext), :] = acci[...]
        row = lax.broadcasted_iota(jnp.int32, (ext, hid), 0)
        out_ref[pl.ds(hid + ext, ext), :] = jnp.where(
            row == feat, accm[pl.ds(hid, ext), :], acco[...]
        )


def closure(sources, feat, w_in, bias_in, w_mid, bias_mid, w_out, out_rows):
    ext, cells = sources.shape
    hid = w_mid.shape[0]
    block = math.gcd(cells, 2048)
    steps = cells // block
    outs = w_out.shape[1]
    w1 = jnp.concatenate([w_in.T, jnp.zeros((hid, ext - feat), jnp.bfloat16)], axis=1)
    wo = jnp.concatenate([jnp.zeros((hid, ext - outs), jnp.bfloat16), w_out], axis=1)
    wi = jnp.concatenate([w_in, jnp.zeros((ext - feat, hid), jnp.bfloat16)], axis=0)
    whole = lambda shape: pl.BlockSpec(shape, lambda i: (0, 0))
    return pl.pallas_call(
        functools.partial(closure_kernel, steps, feat),
        grid=(steps,),
        in_specs=[
            pl.BlockSpec((ext, block), lambda i: (0, i)),
            whole((hid, ext)),
            whole((hid, 1)),
            whole((hid, hid)),
            whole((hid, hid)),
            whole((hid, 1)),
            whole((hid, ext)),
            whole((ext, hid)),
        ],
        out_specs=[
            pl.BlockSpec((feat, block), lambda i: (0, i)),
            whole((out_rows, hid)),
        ],
        out_shape=[
            jax.ShapeDtypeStruct((feat, cells), jnp.float32),
            jax.ShapeDtypeStruct((out_rows, hid), jnp.float32),
        ],
        scratch_shapes=[
            pltpu.VMEM((hid + ext, block), jnp.bfloat16),
            pltpu.VMEM((hid + ext, hid), jnp.float32),
            pltpu.VMEM((ext, hid), jnp.float32),
            pltpu.VMEM((ext, hid), jnp.float32),
        ],
        compiler_params=pltpu.CompilerParams(vmem_limit_bytes=48 << 20),
        name="closure",
    )(sources, w1, bias_in[:, None], w_mid.T, w_mid, bias_mid[:, None], wo, wi)


def reduce_kernel(rows, cols, factor, g_ref, o_ref, rbuf, cbuf, send_r, recv_r, send_c, recv_c,
                  send_o, recv_o):
    me_r, me_c = lax.axis_index("row"), lax.axis_index("col")
    barrier = pltpu.get_barrier_semaphore()
    for d in range(1, rows):
        pl.semaphore_signal(
            barrier, inc=1, device_id=(lax.rem(me_r + d, rows), me_c), device_id_type=MESH
        )
    for d in range(1, cols):
        pl.semaphore_signal(
            barrier, inc=1, device_id=(me_r, lax.rem(me_c + d, cols)), device_id_type=MESH
        )
    pl.semaphore_wait(barrier, rows + cols - 2)
    first = []
    for d in range(1, rows):
        peer = lax.rem(me_r + d, rows)
        copy = pltpu.make_async_remote_copy(
            src_ref=g_ref.at[peer], dst_ref=rbuf.at[d], send_sem=send_r.at[d],
            recv_sem=recv_r.at[d], device_id=(peer, me_c), device_id_type=MESH,
        )
        copy.start()
        first.append(copy)
    total = g_ref[me_r]
    for d in range(1, rows):
        first[d - 1].wait_recv()
        total = total + rbuf[d]
    cbuf[me_c] = total
    second = []
    for d in range(1, cols):
        copy = pltpu.make_async_remote_copy(
            src_ref=cbuf.at[me_c], dst_ref=cbuf.at[me_c], send_sem=send_c.at[d],
            recv_sem=recv_c.at[d], device_id=(me_r, lax.rem(me_c + d, cols)), device_id_type=MESH,
        )
        copy.start()
        second.append(copy)
    for copy in second:
        copy.wait_recv()
    total = cbuf[0]
    for c in range(1, cols):
        total = total + cbuf[c]
    o_ref[me_r] = total * factor
    third = []
    for d in range(1, rows):
        copy = pltpu.make_async_remote_copy(
            src_ref=o_ref.at[me_r], dst_ref=o_ref.at[me_r], send_sem=send_o.at[d],
            recv_sem=recv_o.at[d], device_id=(lax.rem(me_r + d, rows), me_c), device_id_type=MESH,
        )
        copy.start()
        third.append(copy)
    for copy in third:
        copy.wait_recv()
    for copy in first + second + third:
        copy.wait_send()


def reduce_all(grads, rows, cols, factor):
    _, share, width = grads.shape
    dma = pltpu.SemaphoreType.DMA
    return pl.pallas_call(
        functools.partial(reduce_kernel, rows, cols, factor),
        out_shape=jax.ShapeDtypeStruct(grads.shape, jnp.float32),
        in_specs=[pl.BlockSpec(memory_space=pltpu.VMEM)],
        out_specs=pl.BlockSpec(memory_space=pltpu.VMEM),
        scratch_shapes=[
            pltpu.VMEM((rows, share, width), jnp.float32),
            pltpu.VMEM((cols, share, width), jnp.float32),
            dma((rows,)), dma((rows,)), dma((cols,)), dma((cols,)), dma((rows,)), dma((rows,)),
        ],
        compiler_params=pltpu.CompilerParams(collective_id=0, has_side_effects=True),
        name="reduce_all",
    )(grads)


def per_device(features, cotangent, w_in, bias_in, w_mid, bias_mid, w_out, rows, cols):
    stress = spectral(cotangent, rows, cols)
    feat, outs = features.shape[0], w_out.shape[1]
    hid = w_mid.shape[0]
    cells = math.prod(features.shape[1:])
    ext = 16 * (-(-(feat + 1 + outs) // 16))
    sources = jnp.concatenate(
        [
            features.reshape(feat, cells),
            jnp.ones((ext - feat - outs, cells), jnp.bfloat16),
            stress.astype(jnp.bfloat16),
        ],
        axis=0,
    )
    share = 8 * (-(-(hid + 2 * ext) // (8 * rows)))
    field, grads = closure(
        sources, feat, w_in, bias_in, w_mid, bias_mid, w_out, rows * share
    )
    factor = 1.0 / math.sqrt(cells * rows * cols)
    total = reduce_all(grads.reshape(rows, share, hid), rows, cols, factor)
    total = total.reshape(rows * share, hid)
    last = hid + ext
    return (
        field.reshape(features.shape),
        total[hid : hid + feat],
        total[hid + feat],
        total[:hid],
        total[last + feat],
        total[last + ext - outs : last + ext].T,
    )


def solution(mesh):
    body = functools.partial(per_device, rows=mesh.shape["row"], cols=mesh.shape["col"])
    return jax.shard_map(
        body,
        mesh=mesh,
        in_specs=(
            P(None, None, "row", "col", None),
            P(None, None, "row", "col", None),
            P(),
            P(),
            P(),
            P(),
            P(),
        ),
        out_specs=(P(None, None, "row", "col", None), P(), P(), P(), P(), P()),
        check_vma=False,
    )
```

time: 862 us -> 263 us (0.31); the launches traced: 851 us -> 261 us
  matrix products: 241 us -> 11 us
  waiting for transfers between devices: 192 us -> 27.5 us
  local copies, waits for them, and re-layouts: 207 us -> 78.1 us
  blocking collectives: 136 us -> 21.2 us
  Pallas kernels: 0 us -> 104 us
  other arithmetic: 46.9 us -> 4.57 us
  between operations: 14.8 us -> 1.04 us
    dot_general x84 -> x6, matrix products: 241 us -> 11 us  [the longest x4 5.76 us: contract_last(): lax.dot_general(left, right, (((1,), (1,)), ((), ())), precision=HIGHEST,...]
    psum x1 -> x0, waiting for transfers between devices: 125 us -> none  [per_device(): lax.psum((local[0], local[1], local[2], local[3], local[4]), ('row', 'col'))]
    pallas_call x0 -> x2, Pallas kernels: none -> 104 us  [the longest x1 77 us: closure(): pl.pallas_call(functools.partial(closure_kernel, steps, feat), grid=(step...]
    all_to_all x2 -> x1, blocking collectives: 98.2 us -> 21.2 us  [spectral(): part = lax.all_to_all(part.reshape(rows, 2 * bx, ns * ky * kz), 'row', 0, 0)]
    unnamed x35 -> x40, local copies, waits for them, and re-layouts: 76.5 us -> 8.65 us
    another operation x8 -> x1, local copies, waits for them, and re-layouts: 52.6 us -> 2.19 us  [spectral(): part = jnp.stack(sent, axis=2).reshape(2 * kx, ns * ky * kz)]
    all_to_all x2 -> x3, waiting for transfers between devices: 66.9 us -> 27.5 us  [the longest x1 10.3 us: spectral(): part = lax.all_to_all(part.reshape(rows, 2 * ky, kz * nc * bx), 'row', 0, 0)]
    psum x1 -> x0, blocking collectives: 37.4 us -> none  [per_device(): lax.psum((local[0], local[1], local[2], local[3], local[4]), ('row', 'col'))]
  transfers between devices with their start and end apart: 3 -> 3, of which waited for: 3 -> 3; matrix products, arithmetic and copies ran while one was open for 0% -> 2% of each run, Pallas kernels for 0% -> 0%
where the time goes in v1:
time: 263 us; the launch traced here: 261 us
  Pallas kernels  104 us (40%)
  local copies, waits for them, and re-layouts  78.1 us (30%)
  waiting for transfers between devices  27.5 us (10%)
  blocking collectives  21.2 us (8%)
  starting transfers between devices  14.2 us (5%)
  matrix products  11 us (4%)
  other arithmetic  4.57 us (2%)
    pallas_call x1, Pallas kernels, closure(): pl.pallas_call(functools.partial(closure_kernel, steps, feat), grid=(step...  77 us
    pallas_call x1, Pallas kernels, reduce_all(): pl.pallas_call(functools.partial(reduce_kernel, rows, cols, factor), out_...  26.7 us
    all_to_all x1, blocking collectives, spectral(): part = lax.all_to_all(part.reshape(rows, 2 * bx, ns * ky * kz), 'row', 0, 0)  21.2 us
    transpose x1, local copies, waits for them, and re-layouts, spectral(): part = part.reshape(rows, 2, bx, ns, ky, kz).transpose(2, 3, 5, 1, 0, 4)  12.2 us
    all_to_all x1, waiting for transfers between devices, spectral(): part = lax.all_to_all(part.reshape(rows, 2 * ky, kz * nc * bx), 'row', 0, 0)  10.3 us
    all_to_all x1, waiting for transfers between devices, spectral(): part = lax.all_to_all(part.reshape(cols, 2 * by, bx * ns * kz), 'col', 0, 0)  9.4 us
    unnamed x40, local copies, waits for them, and re-layouts  8.65 us
    all_to_all x1, waiting for transfers between devices, spectral(): part = lax.all_to_all(part.reshape(cols, 2 * kz, nc * bx * by), 'col', 0, 0)  7.88 us
  transfers between devices with their start and end apart: 3, of which 3 were waited for; matrix products, arithmetic and copies ran while one was open for 2% of the time, Pallas kernels for 0%

profile of v1, /device:TPU:25, one launch (start us, length us, event | category | flops | bytes accessed | tf_op | source)
XLA Modules:
  0.0 261.4 jit_solution(9787863924670694047)
XLA Ops:
  0.6 1.1 copy-done
  1.8 2.5 fusion.5
  4.3 3.5 %all-to-all-start = ((f32[4,22,1536]{2,1,0:T(8,128)}), f32[4,22,1536]{2,1,0:T(8,128)S(1)}, u32[]{:S(2)}, u32[]{:S(2)}) async-start(f32[4,22,1536]{2,1,0:T(8,128)} %fusion.5), calls=%async_computation | async-start | bytes 1179648 | tf_op jit(solution)/shard_map/all_to_all | solution.py:71
  7.8 7.9 %all-to-all-done = f32[4,22,1536]{2,1,0:T(8,128)S(1)} async-done(((f32[4,22,1536]{2,1,0:T(8,128)}), f32[4,22,1536]{2,1,0:T(8,128)S(1)}, u32[]{:S(2)}, u32[]{:S(2)}) %all-to-all-start) | async-done | bytes 540704 | tf_op jit(solution)/shard_map/all_to_all | solution.py:71
  15.7 0.3 copy.26
  16.0 0.7 reshape.196
  16.7 2.2 copy.27
  18.9 2.9 %reshape.197 = f32[528,256]{1,0:T(8,128)S(1)} reshape(f32[11,3,16,2,4,32]{5,4,3,2,1,0:T(4,128)} %copy.27) | data formatting | bytes 1081344 | tf_op jit(solution)/shard_map/reshape | solution.py:73
  21.8 0.8 fusion.6
  22.6 0.8 reshape.198
  23.4 6.5 %all-to-all-start.1 = ((f32[8,22,528]{2,1,0:T(8,128)}), f32[8,22,528]{2,1,0:T(8,128)S(1)}, u32[]{:S(2)}, u32[]{:S(2)}) async-start(f32[8,22,528]{2,1,0:T(8,128)} %reshape.198), calls=%async_computation.1 | async-start | bytes 983040 | tf_op jit(solution)/shard_map/all_to_all | solution.py:77
  29.9 0.7 dynamic-slice_bitcast_fusion.1
  30.8 0.7 dynamic-slice_bitcast_fusion
  31.7 10.3 %all-to-all-done.1 = f32[8,22,528]{2,1,0:T(8,128)S(1)} async-done(((f32[8,22,528]{2,1,0:T(8,128)}), f32[8,22,528]{2,1,0:T(8,128)S(1)}, u32[]{:S(2)}, u32[]{:S(2)}) %all-to-all-start.1) | async-done | bytes 371744 | tf_op jit(solution)/shard_map/all_to_all | solution.py:77
  42.0 3.5 %reshape.199 = f32[8,2,11,11,3,16]{5,4,3,0,2,1:T(4,128)} reshape(f32[8,22,528]{2,0,1:T(8,128)S(1)} %copy.28) | data formatting | bytes 743424 | tf_op jit(solution)/shard_map/reshape | solution.py:78
  45.5 4.0 %copy.29 = f32[3,11,11,2,8,16]{5,4,3,2,1,0:T(8,128)} copy(f32[3,11,11,2,8,16]{5,0,2,4,1,3:T(4,128)} %bitcast.73) | data formatting | bytes 743424 | tf_op jit(solution)/shard_map/transpose | solution.py:78
  49.5 2.8 %reshape.200 = f32[363,256]{1,0:T(8,128)S(1)} reshape(f32[3,11,11,2,8,16]{5,4,3,2,1,0:T(8,128)} %copy.29) | data formatting | bytes 743424 | tf_op jit(solution)/shard_map/reshape | solution.py:79
  52.4 0.5 fusion.7
  53.1 0.5 add_multiply_fusion
  53.7 0.3 add_multiply_fusion.1
  54.2 2.2 stack.2
  56.6 0.8 fusion.8
  57.4 21.2 %all_to_all.20 = f32[8,32,605]{2,1,0:T(8,128)} all-to-all(f32[8,32,605]{2,1,0:T(8,128)S(1)} %bitcast.80), channel_id=1, replica_groups=mesh['row'=8,'col'=4] {'row'}, dimensions={0} | all-to-all | bytes 1239040 | tf_op jit(solution)/shard_map/all_to_all | solution.py:106
  78.6 2.0 copy.31
  80.7 4.9 %reshape.204 = f32[8,2,16,5,11,11]{2,1,0,5,4,3:T(2,128)} reshape(f32[8,32,605]{1,0,2:T(8,128)S(1)} %copy.31) | data formatting | bytes 1239040 | tf_op jit(solution)/shard_map/reshape | solution.py:107
  85.6 12.2 %copy.32 = f32[16,5,11,2,8,11]{5,4,3,2,1,0:T(8,128)} copy(f32[16,5,11,2,8,11]{0,3,4,2,5,1:T(2,128)} %bitcast.72) | data formatting | bytes 1239040 | tf_op jit(solution)/shard_map/transpose | solution.py:107
  97.8 5.6 %reshape.205 = f32[880,176]{1,0:T(8,128)S(1)} reshape(f32[16,5,11,2,8,11]{5,4,3,2,1,0:T(8,128)} %copy.32) | data formatting | bytes 1239040 | tf_op jit(solution)/shard_map/reshape | solution.py:108
  103.4 2.0 fusion.9
  105.4 4.2 %all-to-all-start.3 = ((f32[4,64,880]{2,1,0:T(8,128)}), f32[4,64,880]{2,1,0:T(8,128)}, u32[]{:S(2)}, u32[]{:S(2)}) async-start(f32[4,64,880]{2,1,0:T(8,128)} %bitcast.8), calls=%async_computation.3 | async-start | bytes 1835008 | tf_op jit(solution)/shard_map/all_to_all | solution.py:112
  110.1 1.4 copy.44
  112.2 9.4 %all-to-all-done.3 = f32[4,64,880]{2,1,0:T(8,128)} async-done(((f32[4,64,880]{2,1,0:T(8,128)}), f32[4,64,880]{2,1,0:T(8,128)}, u32[]{:S(2)}, u32[]{:S(2)}) %all-to-all-start.3) | async-done | bytes 901152 | tf_op jit(solution)/shard_map/all_to_all | solution.py:112
  121.6 2.9 %copy.34 = f32[4,64,880]{1,2,0:T(8,128)} copy(f32[4,64,880]{2,1,0:T(8,128)} %all-to-all-done.3) | data formatting | bytes 1802240 | tf_op jit(solution)/shard_map/all_to_all | solution.py:112
  124.5 4.7 %reshape.207 = f32[4,2,32,16,5,11]{2,1,5,4,3,0:T(2,128)} reshape(f32[4,64,880]{1,2,0:T(8,128)} %copy.34) | data formatting | bytes 1802240 | tf_op jit(solution)/shard_map/reshape | solution.py:113
  129.2 4.1 %copy.35 = f32[5,16,32,2,4,11]{2,1,0,5,4,3:T(8,128)} copy(f32[5,16,32,2,4,11]{2,3,5,0,1,4:T(2,128)} %bitcast.74) | data formatting | bytes 1802240 | tf_op jit(solution)/shard_map/transpose | solution.py:113
  133.3 3.7 %reshape.208 = f32[2560,88]{0,1:T(8,128)} reshape(f32[5,16,32,2,4,11]{2,1,0,5,4,3:T(8,128)} %copy.35) | data formatting | bytes 1802240 | tf_op jit(solution)/shard_map/reshape | solution.py:114
  137.0 4.5 %fusion.4 = (bf16[2560,128]{1,0:T(8,128)(2,1)S(1)}, f32[2560,128]{1,0:T(8,128)}) fusion(f32[2560,88]{0,1:T(8,128)} %reshape.208, f32[88,128]{1,0:T(8,128)S(1)} %copy-done.9), kind=kOutput, calls=%fused_computation.24 | convolution fusion | flops 346357760 | bytes 2912256 | tf_op jit(solution)/shard_map/dot_general | solution.py:117
  141.5 1.7 reshape.209
  143.2 1.1 fusion.2
  144.5 2.3 pad_maximum_fusion.s_ref
  146.8 77.0 %closure.1 = (f32[9,65536]{1,0:T(8,128)}, f32[320,256]{1,0:T(8,128)S(1)}) custom-call(bf16[16,65536]{1,0:T(8,128)(2,1)S(1)} %pad_maximum_fusion.s_ref, bf16[256,16]{1,0:T(8,128)(2,1)S(1)} %concatenate.16.w1_ref, f32[256,1]{1,0:T(8,128)S(1)} %copy.39.b1_ref, bf16[256,256]{1,0:T(8,128)(2,1)S(1)} %bitcast.70, bf16[256,256]{1,0:T(8,128)(2,1)S(1)} %copy-done.2, ...), custom_call_target="tpu_custom_call" | custom-call | tf_op jit(solution)/shard_map/closure/pallas_call | solution.py:179
  223.7 0.7 copy-done.3
  224.5 26.7 %reduce_all.1 = f32[8,40,256]{2,1,0:T(8,128)} custom-call(f32[8,40,256]{2,1,0:T(8,128)} %bitcast.71), custom_call_target="tpu_custom_call" | custom-call | tf_op jit(solution)/shard_map/reduce_all/pallas_call | solution.py:269
  251.2 1.7 slice.49
  252.9 1.3 slice.47
  254.2 1.3 slice_bitcast_fusion
  255.5 1.3 fusion.3
  256.8 3.0 %copy.46 = f32[2,8,512,128]{3,2,1,0:T(8,128)S(1)} copy(f32[2,8,512,128]{3,1,2,0:T(8,128)} %bitcast.79) | data formatting | bytes 8388608
  259.8 1.6 slice.52
  (53 shorter events, 2.4 us)
Async XLA Ops:
  0.6 1.1 copy-start
  4.3 11.4 %all-to-all-start = ((f32[4,22,1536]{2,1,0:T(8,128)}), f32[4,22,1536]{2,1,0:T(8,128)S(1)}, u32[]{:S(2)}, u32[]{:S(2)}) async-start(f32[4,22,1536]{2,1,0:T(8,128)} %fusion.5), calls=%async_computation | async-start | bytes 1179648 | tf_op jit(solution)/shard_map/all_to_all | solution.py:71
  18.9 2.9 %copy-start.7 = (f32[176,256]{1,0:T(8,128)S(1)}, f32[176,256]{1,0:T(8,128)}, u32[]{:S(2)}) copy-start(f32[176,256]{1,0:T(8,128)} %constant.57.clone) | copy-start | bytes 540676
  18.9 12.6 %copy-start.15 = (f32[85]{0:T(128)S(1)}, f32[85]{0:T(128)}, u32[]{:S(2)}) copy-start(f32[85]{0:T(128)} %constant.75) | copy-start | bytes 1024
  23.4 18.5 %all-to-all-start.1 = ((f32[8,22,528]{2,1,0:T(8,128)}), f32[8,22,528]{2,1,0:T(8,128)S(1)}, u32[]{:S(2)}, u32[]{:S(2)}) async-start(f32[8,22,528]{2,1,0:T(8,128)} %reshape.198), calls=%async_computation.1 | async-start | bytes 983040 | tf_op jit(solution)/shard_map/all_to_all | solution.py:77
  49.5 2.8 %copy-start.8 = (f32[170,256]{1,0:T(8,128)S(1)}, f32[170,256]{1,0:T(8,128)}, u32[]{:S(2)}) copy-start(f32[170,256]{1,0:T(8,128)} %constant.58.clone) | copy-start | bytes 522244
  49.5 3.6 %copy-start.11 = (f32[85]{0:T(128)S(1)}, f32[85]{0:T(128)}, u32[]{:S(2)}) copy-start(f32[85]{0:T(128)} %constant.59.clone) | copy-start | bytes 1024
  52.9 3.7 %copy-start.5 = (f32[256,170]{1,0:T(8,128)S(1)}, f32[256,170]{1,0:T(8,128)}, u32[]{:S(2)}) copy-start(f32[256,170]{1,0:T(8,128)} %constant.62.clone) | copy-start | bytes 522244
  97.8 5.6 %copy-start.6 = (f32[256,176]{1,0:T(8,128)S(1)}, f32[256,176]{1,0:T(8,128)}, u32[]{:S(2)}) copy-start(f32[256,176]{1,0:T(8,128)} %constant.63.clone) | copy-start | bytes 540676
  103.4 6.2 %copy-start.10 = (bf16[9,256]{1,0:T(8,128)(2,1)S(1)}, bf16[9,256]{1,0:T(8,128)(2,1)}, u32[]{:S(2)}) copy-start(bf16[9,256]{1,0:T(8,128)(2,1)} %param.18) | copy-start | bytes 13828
  103.4 6.4 %copy-start.4 = (bf16[9,1,16,32,128]{4,3,2,1,0:T(8,128)(2,1)S(1)}, bf16[9,1,16,32,128]{4,3,2,1,0:T(8,128)(2,1)}, u32[]{:S(2)}) copy-start(bf16[9,1,16,32,128]{4,3,2,1,0:T(8,128)(2,1)} %param.16) | copy-start | bytes 3538948
  105.4 16.2 %all-to-all-start.3 = ((f32[4,64,880]{2,1,0:T(8,128)}), f32[4,64,880]{2,1,0:T(8,128)}, u32[]{:S(2)}, u32[]{:S(2)}) async-start(f32[4,64,880]{2,1,0:T(8,128)} %bitcast.8), calls=%async_computation.3 | async-start | bytes 1835008 | tf_op jit(solution)/shard_map/all_to_all | solution.py:112
  110.0 1.4 copy-start.2
  110.0 1.5 copy-start.12
  110.0 1.8 copy-start.13
  110.1 1.9 copy-start.14
  133.3 3.7 %copy-start.9 = (f32[88,128]{1,0:T(8,128)S(1)}, f32[88,128]{1,0:T(8,128)}, u32[]{:S(2)}) copy-start(f32[88,128]{1,0:T(8,128)} %constant.64.clone) | copy-start | bytes 135172
  223.7 0.7 copy-start.3
  259.8 1.6 copy-start.1

commit v2 on v1

--- a/solution.py
+++ b/solution.py
@@ -54,6 +54,50 @@
 
 def f32(a):
     return jnp.asarray(np.ascontiguousarray(a), jnp.float32)
+
+
+def exchange_kernel(axis, x_ref, o_ref, send, recv, local):
+    me_r, me_c = lax.axis_index("row"), lax.axis_index("col")
+    me = me_r if axis == "row" else me_c
+    parts = x_ref.shape[0]
+
+    def device(index):
+        return (index, me_c) if axis == "row" else (me_r, index)
+
+    barrier = pltpu.get_barrier_semaphore()
+    for d in range(1, parts):
+        pl.semaphore_signal(
+            barrier, inc=1, device_id=device(lax.rem(me + d, parts)), device_id_type=MESH
+        )
+    own = pltpu.make_async_copy(x_ref.at[me], o_ref.at[me], local)
+    own.start()
+    pl.semaphore_wait(barrier, parts - 1)
+    copies = []
+    for d in range(1, parts):
+        peer = lax.rem(me + d, parts)
+        copy = pltpu.make_async_remote_copy(
+            src_ref=x_ref.at[peer], dst_ref=o_ref.at[me], send_sem=send.at[d],
+            recv_sem=recv.at[d], device_id=device(peer), device_id_type=MESH,
+        )
+        copy.start()
+        copies.append(copy)
+    own.wait()
+    for copy in copies:
+        copy.wait()
+
+
+def exchange(x, axis, ident):
+    parts = x.shape[0]
+    dma = pltpu.SemaphoreType.DMA
+    return pl.pallas_call(
+        functools.partial(exchange_kernel, axis),
+        out_shape=jax.ShapeDtypeStruct(x.shape, x.dtype),
+        in_specs=[pl.BlockSpec(memory_space=pl.ANY)],
+        out_specs=pl.BlockSpec(memory_space=pl.ANY),
+        scratch_shapes=[dma((parts,)), dma((parts,)), dma(())],
+        compiler_params=pltpu.CompilerParams(collective_id=ident, has_side_effects=True),
+        name="exchange_" + axis,
+    )(x)
 
 
 def spectral(cotangent, rows, cols):
@@ -68,13 +112,13 @@
     az = angles(mz, nz)
     table = np.stack([np.cos(az), -np.sin(az)], 1) * live_z[:, None, :, None]
     part = contract_last(f32(table.reshape(cols * 2 * kz, nz)), cotangent.reshape(nc * bx * by, nz))
-    part = lax.all_to_all(part.reshape(cols, 2 * kz, nc * bx * by), "col", 0, 0)
+    part = exchange(part.reshape(cols, 2 * kz, nc * bx * by), "col", 1)
     part = part.reshape(cols, 2, kz, nc, bx, by).transpose(2, 3, 4, 1, 0, 5)
     part = part.reshape(kz * nc * bx, 2 * ny)
     table = forward_complex(my, live_y, ny)
     table = table.transpose(0, 2, 1, 3, 4).reshape(rows * 2 * ky, 2 * ny)
     part = contract_last(f32(table), part)
-    part = lax.all_to_all(part.reshape(rows, 2 * ky, kz * nc * bx), "row", 0, 0)
+    part = exchange(part.reshape(rows, 2 * ky, kz * nc * bx), "row", 2)
     part = part.reshape(rows, 2, ky, kz, nc, bx).transpose(4, 2, 3, 1, 0, 5)
     part = part.reshape(nc * ky * kz, 2 * nx)
     table = forward_complex(mx, np.ones(kx), nx)
@@ -96,97 +140,102 @@
     sent = []
     for a, b in ((1, 1), (2, 2), (0, 1), (0, 2), (1, 2)):
         value = waves[a] * proj[a] if a == b else waves[b] * proj[a] + waves[a] * proj[b]
-        sent.append(STEP_DT * value)
+        sent.append((STEP_DT * value).reshape(2 * kx, ky, kz))
     ns = len(sent)
-    part = jnp.stack(sent, axis=2).reshape(2 * kx, ns * ky * kz)
+    wide = 2 ** math.ceil(math.log2(ns * kz))
+    part = jnp.concatenate(sent + [jnp.zeros((2 * kx, ky, wide - ns * kz), jnp.float32)], axis=2)
+    part = part.reshape(2 * kx, ky * wide)
     table = inverse_complex(mx, np.ones(kx), nx)
     table = np.stack([table[:, :, 1], -table[:, :, 0]], 2)
     table = table.reshape(kx, 2, 2, rows, bx).transpose(3, 1, 4, 2, 0).reshape(rows * 2 * bx, 2 * kx)
     part = jnp.dot(f32(table), part, precision=HIGHEST, preferred_element_type=jnp.float32)
-    part = lax.all_to_all(part.reshape(rows, 2 * bx, ns * ky * kz), "row", 0, 0)
-    part = part.reshape(rows, 2, bx, ns, ky, kz).transpose(2, 3, 5, 1, 0, 4)
-    part = part.reshape(bx * ns * kz, 2 * rows * ky)
+    part = exchange(part.reshape(rows, 2 * bx, ky * wide), "row", 3)
+    part = part.reshape(rows * 2, bx, ky, wide).transpose(0, 2, 1, 3)
+    part = part.reshape(rows * 2 * ky, bx * wide)
     table = inverse_complex(my, live_y, ny)
-    table = table.reshape(rows, ky, 2, 2, cols, by).transpose(4, 2, 5, 3, 0, 1)
-    part = contract_last(f32(table.reshape(cols * 2 * by, 2 * rows * ky)), part)
-    part = lax.all_to_all(part.reshape(cols, 2 * by, bx * ns * kz), "col", 0, 0)
-    part = part.reshape(cols, 2, by, bx, ns, kz).transpose(4, 3, 2, 1, 0, 5)
-    part = part.reshape(ns * bx * by, 2 * cols * kz)
+    table = table.reshape(rows, ky, 2, 2, cols, by).transpose(4, 2, 5, 0, 3, 1)
+    table = f32(table.reshape(cols * 2 * by, rows * 2 * ky))
+    part = jnp.dot(table, part, precision=HIGHEST, preferred_element_type=jnp.float32)
+    part = exchange(part.reshape(cols, 2 * by, bx * wide), "col", 4)
+    part = part.reshape(cols * 2, by, bx, wide).transpose(2, 1, 0, 3)
+    part = part.reshape(bx * by, cols * 2 * wide)
     weight = np.where(mz == 0, 1.0, 2.0) * live_z / nz
-    table = np.stack([np.cos(az), -np.sin(az)], 0) * weight[None, :, :, None]
+    table = np.stack([np.cos(az), -np.sin(az)], 1) * weight[:, None, :, None]
+    full = np.zeros((cols, 2, wide, ns + 1, nz))
+    for comp in range(ns):
+        full[:, :, comp * kz : (comp + 1) * kz, comp + 1] = table
+    full[:, :, :, 0] = -(full[:, :, :, 1] + full[:, :, :, 2])
     part = jnp.dot(
         part,
-        f32(table.reshape(2 * cols * kz, nz)),
+        f32(full.reshape(cols * 2 * wide, (ns + 1) * nz)),
         precision=HIGHEST,
         preferred_element_type=jnp.float32,
-    ).reshape(ns, bx * by * nz)
-    return jnp.concatenate([-(part[0:1] + part[1:2]), part], axis=0)
+    )
+    return part.reshape(bx * by, ns + 1, nz).transpose(1, 0, 2).reshape(ns + 1, bx * by * nz)
 
 
 def closure_kernel(steps, feat, s_ref, w1_ref, b1_ref, w2t_ref, w2_ref, b2_ref, wo_ref, wi_ref,
-                   gx_ref, out_ref, left, accm, acci, acco):
+                   gx_ref, out_ref, accm, acci, acco, accb):
     step = pl.program_id(0)
     hid = w2_ref.shape[0]
     ext = s_ref.shape[0]
-    trans = (((1,), (1,)), ((), ()))
+    first = (((0,), (0,)), ((), ()))
+    last = (((1,), (1,)), ((), ()))
 
     @pl.when(step == 0)
     def _():
         accm[...] = jnp.zeros_like(accm)
         acci[...] = jnp.zeros_like(acci)
         acco[...] = jnp.zeros_like(acco)
+        accb[...] = jnp.zeros_like(accb)
 
     s = s_ref[...]
-    left[pl.ds(hid, ext), :] = s
-    pre = jnp.dot(w1_ref[...], s, preferred_element_type=jnp.float32) + b1_ref[...]
+    pre = lax.dot_general(s, w1_ref[...], first, preferred_element_type=jnp.float32) + b1_ref[...]
     act_in = jnp.tanh(pre).astype(jnp.bfloat16)
-    left[pl.ds(0, hid), :] = act_in
-    pre = jnp.dot(w2t_ref[...], act_in, preferred_element_type=jnp.float32) + b2_ref[...]
+    pre = jnp.dot(act_in, w2_ref[...], preferred_element_type=jnp.float32) + b2_ref[...]
     act_mid = jnp.tanh(pre).astype(jnp.bfloat16)
     wide = act_mid.astype(jnp.float32)
-    back = jnp.dot(wo_ref[...], s, preferred_element_type=jnp.float32)
+    back = lax.dot_general(s, wo_ref[...], first, preferred_element_type=jnp.float32)
     delta_mid = (back * (1.0 - wide * wide)).astype(jnp.bfloat16)
-    acco[...] += lax.dot_general(s, act_mid, trans, preferred_element_type=jnp.float32)
-    accm[...] += lax.dot_general(left[...], delta_mid, trans, preferred_element_type=jnp.float32)
-    back = jnp.dot(w2_ref[...], delta_mid, preferred_element_type=jnp.float32)
-    wide = left[pl.ds(0, hid), :].astype(jnp.float32)
+    accb[...] += jnp.sum(delta_mid.astype(jnp.float32), axis=0, keepdims=True)
+    acco[...] += jnp.dot(s, act_mid, preferred_element_type=jnp.float32)
+    accm[...] += lax.dot_general(act_in, delta_mid, first, preferred_element_type=jnp.float32)
+    back = jnp.dot(delta_mid, w2t_ref[...], preferred_element_type=jnp.float32)
+    wide = act_in.astype(jnp.float32)
     delta_in = (back * (1.0 - wide * wide)).astype(jnp.bfloat16)
-    acci[...] += lax.dot_general(s, delta_in, trans, preferred_element_type=jnp.float32)
-    grad = jnp.dot(wi_ref[...], delta_in, preferred_element_type=jnp.float32)
+    acci[...] += jnp.dot(s, delta_in, preferred_element_type=jnp.float32)
+    grad = lax.dot_general(wi_ref[...], delta_in, last, preferred_element_type=jnp.float32)
     gx_ref[...] = grad[:feat]
 
     @pl.when(step == steps - 1)
     def _():
         out_ref[...] = jnp.zeros_like(out_ref)
-        out_ref[pl.ds(0, hid), :] = accm[pl.ds(0, hid), :]
+        out_ref[pl.ds(0, hid), :] = accm[...]
         out_ref[pl.ds(hid, ext), :] = acci[...]
         row = lax.broadcasted_iota(jnp.int32, (ext, hid), 0)
-        out_ref[pl.ds(hid + ext, ext), :] = jnp.where(
-            row == feat, accm[pl.ds(hid, ext), :], acco[...]
-        )
+        out_ref[pl.ds(hid + ext, ext), :] = jnp.where(row == feat, accb[...], acco[...])
 
 
 def closure(sources, feat, w_in, bias_in, w_mid, bias_mid, w_out, out_rows):
     ext, cells = sources.shape
     hid = w_mid.shape[0]
-    block = math.gcd(cells, 2048)
+    block = math.gcd(cells, 4096)
     steps = cells // block
     outs = w_out.shape[1]
-    w1 = jnp.concatenate([w_in.T, jnp.zeros((hid, ext - feat), jnp.bfloat16)], axis=1)
-    wo = jnp.concatenate([jnp.zeros((hid, ext - outs), jnp.bfloat16), w_out], axis=1)
     wi = jnp.concatenate([w_in, jnp.zeros((ext - feat, hid), jnp.bfloat16)], axis=0)
+    wo = jnp.concatenate([jnp.zeros((ext - outs, hid), jnp.bfloat16), w_out.T], axis=0)
     whole = lambda shape: pl.BlockSpec(shape, lambda i: (0, 0))
     return pl.pallas_call(
         functools.partial(closure_kernel, steps, feat),
         grid=(steps,),
         in_specs=[
             pl.BlockSpec((ext, block), lambda i: (0, i)),
-            whole((hid, ext)),
-            whole((hid, 1)),
+            whole((ext, hid)),
+            whole((1, hid)),
             whole((hid, hid)),
             whole((hid, hid)),
-            whole((hid, 1)),
-            whole((hid, ext)),
+            whole((1, hid)),
+            whole((ext, hid)),
             whole((ext, hid)),
         ],
         out_specs=[
@@ -198,14 +247,14 @@
             jax.ShapeDtypeStruct((out_rows, hid), jnp.float32),
         ],
         scratch_shapes=[
-            pltpu.VMEM((hid + ext, block), jnp.bfloat16),
-            pltpu.VMEM((hid + ext, hid), jnp.float32),
+            pltpu.VMEM((hid, hid), jnp.float32),
             pltpu.VMEM((ext, hid), jnp.float32),
             pltpu.VMEM((ext, hid), jnp.float32),
+            pltpu.VMEM((1, hid), jnp.float32),
         ],
         compiler_params=pltpu.CompilerParams(vmem_limit_bytes=48 << 20),
         name="closure",
-    )(sources, w1, bias_in[:, None], w_mid.T, w_mid, bias_mid[:, None], wo, wi)
+    )(sources, wi, bias_in[None], w_mid.T, w_mid, bias_mid[None], wo, wi)
 
 
 def reduce_kernel(rows, cols, factor, g_ref, o_ref, rbuf, cbuf, send_r, recv_r, send_c, recv_c,

time: 263 us -> 219 us (0.83)
  Pallas kernels: 104 us -> 155 us
  local copies, waits for them, and re-layouts: 78.1 us -> 48.3 us
  waiting for transfers between devices: 27.5 us -> 0 us
  blocking collectives: 21.2 us -> 0 us
  starting transfers between devices: 14.2 us -> 0 us
    pallas_call x0 -> x4, Pallas kernels: none -> 60.3 us  [exchange(): pl.pallas_call(functools.partial(exchange_kernel, axis), out_shape=jax.Sh...]
    all_to_all x3 -> x0, waiting for transfers between devices: 27.5 us -> none  [the longest x1 10.3 us: spectral(): part = lax.all_to_all(part.reshape(rows, 2 * ky, kz * nc * bx), 'row', 0, 0)]
    all_to_all x1 -> x0, blocking collectives: 21.2 us -> none  [spectral(): part = lax.all_to_all(part.reshape(rows, 2 * bx, ns * ky * kz), 'row', 0, 0)]
    all_to_all x3 -> x0, starting transfers between devices: 14.2 us -> none  [the longest x1 6.49 us: spectral(): part = lax.all_to_all(part.reshape(rows, 2 * ky, kz * nc * bx), 'row', 0, 0)]
    reshape x8 -> x5, local copies, waits for them, and re-layouts: 21.8 us -> 8.12 us  [the longest x1 2.05 us: spectral(): part = part.reshape(bx * by, cols * 2 * wide)]
    transpose x2, local copies, waits for them, and re-layouts: 16.2 us -> 4.1 us  [the longest x1 2.54 us: spectral(): part = part.reshape(cols * 2, by, bx, wide).transpose(2, 1, 0, 3)]
    pallas_call x1, Pallas kernels: 77 us -> 69.6 us  [closure(): pl.pallas_call(functools.partial(closure_kernel, steps, feat), grid=(step...]
    all_to_all x4 -> x0, local copies, waits for them, and re-layouts: 5.39 us -> none  [the longest x1 2.93 us: spectral(): part = lax.all_to_all(part.reshape(cols, 2 * by, bx * ns * kz), 'col', 0, 0)]
  transfers between devices with their start and end apart: 3 -> 0, of which waited for: 3 -> 0; matrix products, arithmetic and copies ran while one was open for 2% -> 0% of each run, Pallas kernels for 0% -> 0%
where the time goes in v2:
time: 219 us; the launch traced here: 218 us
  Pallas kernels  155 us (71%)
  local copies, waits for them, and re-layouts  48.3 us (22%)
  matrix products  10.2 us (5%)
  other arithmetic  4.22 us (2%)
    pallas_call x1, Pallas kernels, closure(): pl.pallas_call(functools.partial(closure_kernel, steps, feat), grid=(step...  69.6 us
    pallas_call x4, Pallas kernels, exchange(): pl.pallas_call(functools.partial(exchange_kernel, axis), out_shape=jax.Sh...  60.3 us
    pallas_call x1, Pallas kernels, reduce_all(): pl.pallas_call(functools.partial(reduce_kernel, rows, cols, factor), out_...  24.6 us
    unnamed x36, local copies, waits for them, and re-layouts  7.08 us

profile of v2, /device:TPU:25, one launch (start us, length us, event | category | flops | bytes accessed | tf_op | source)
XLA Modules:
  0.0 218.3 jit_solution(1193601058501681827)
XLA Ops:
  0.7 0.8 multiply_compare_fusion
  1.6 0.2 broadcast_in_dim.57
  2.0 0.7 dynamic-slice_bitcast_fusion
  2.7 0.7 fusion.1
  3.5 0.7 fusion.2
  4.3 0.8 add_maximum_fusion
  5.1 0.8 div.31
  5.9 2.5 %fusion.5.x_ref = f32[4,22,1536]{2,1,0:T(8,128)} fusion(f32[4,22,128]{2,1,0:T(8,128)} %constant.72, f32[1536,128,1]{1,0,2:T(8,128)S(1)} %bitcast.82), kind=kOutput, calls=%fused_computation.24 | convolution fusion | flops 207618048 | bytes 1372160 | tf_op jit(solution)/shard_map/dot_general | solution.py:50
  8.5 10.3 %exchange_col.2 = f32[4,22,1536]{2,1,0:T(8,128)} custom-call(f32[4,22,1536]{2,1,0:T(8,128)} %fusion.5.x_ref), custom_call_target="tpu_custom_call" | custom-call | tf_op jit(solution)/shard_map/exchange_col/pallas_call | solution.py:92
  18.8 1.4 copy.26
  20.2 0.7 reshape.265
  20.9 2.2 %copy.27 = f32[11,3,16,2,4,32]{5,4,3,2,1,0:T(4,128)} copy(f32[11,3,16,2,4,32]{5,2,1,4,0,3:T(8,128)S(1)} %bitcast.89) | data formatting | bytes 1081344 | tf_op jit(solution)/shard_map/transpose | solution.py:116
  23.1 2.9 %reshape.266 = f32[528,256]{1,0:T(8,128)S(1)} reshape(f32[11,3,16,2,4,32]{5,4,3,2,1,0:T(4,128)} %copy.27) | data formatting | bytes 1081344 | tf_op jit(solution)/shard_map/reshape | solution.py:117
  26.0 0.8 fusion.6
  26.7 0.8 reshape.267.x_ref
  27.6 14.8 %exchange_row.2 = f32[8,22,528]{2,1,0:T(8,128)} custom-call(f32[8,22,528]{2,1,0:T(8,128)} %reshape.267.x_ref), custom_call_target="tpu_custom_call" | custom-call | tf_op jit(solution)/shard_map/exchange_row/pallas_call | solution.py:92
  42.4 1.1 copy.28
  43.5 3.5 %reshape.268 = f32[8,2,11,11,3,16]{5,4,3,0,2,1:T(4,128)} reshape(f32[8,22,528]{2,0,1:T(8,128)S(1)} %copy.28) | data formatting | bytes 743424 | tf_op jit(solution)/shard_map/reshape | solution.py:122
  47.0 4.0 %copy.29 = f32[3,11,11,2,8,16]{5,4,3,2,1,0:T(8,128)} copy(f32[3,11,11,2,8,16]{5,0,2,4,1,3:T(4,128)} %bitcast.87) | data formatting | bytes 743424 | tf_op jit(solution)/shard_map/transpose | solution.py:122
  51.0 2.8 %reshape.269 = f32[363,256]{1,0:T(8,128)S(1)} reshape(f32[3,11,11,2,8,16]{5,4,3,2,1,0:T(8,128)} %copy.29) | data formatting | bytes 743424 | tf_op jit(solution)/shard_map/reshape | solution.py:123
  53.8 0.5 fusion.7
  54.4 0.2 reshape.270
  54.6 0.2 fusion.3
  55.7 0.2 add_multiply_fusion
  56.2 1.2 concatenate.12
  57.4 1.7 fusion.8
  59.1 20.7 %exchange_row.3 = f32[8,32,704]{2,1,0:T(8,128)} custom-call(f32[8,32,704]{2,1,0:T(8,128)} %bitcast.97), custom_call_target="tpu_custom_call" | custom-call | tf_op jit(solution)/shard_map/exchange_row/pallas_call | solution.py:92
  79.8 1.6 reshape.273
  81.4 1.6 copy.34
  82.9 1.8 reshape.274
  84.7 2.0 fusion.9
  86.7 14.6 %exchange_col.3 = f32[4,64,1024]{2,1,0:T(8,128)} custom-call(f32[4,64,1024]{2,1,0:T(8,128)} %bitcast.95), custom_call_target="tpu_custom_call" | custom-call | tf_op jit(solution)/shard_map/exchange_col/pallas_call | solution.py:92
  101.3 1.9 reshape.276
  103.2 2.5 %copy.35 = f32[16,32,8,64]{3,2,1,0:T(8,128)} copy(f32[16,32,8,64]{3,0,1,2:T(8,128)S(1)} %bitcast.92) | data formatting | bytes 2097152 | tf_op jit(solution)/shard_map/transpose | solution.py:160
  105.7 2.0 reshape.283
  107.8 2.7 %fusion = bf16[1,6,512,128]{3,2,1,0:T(8,128)(2,1)S(1)} fusion(f32[512,512,1]{1,0,2:T(8,128)S(1)} %reshape.283, f32[6,128,512]{2,1,0:T(8,128)S(1)} %copy-done.6), kind=kOutput, calls=%fused_computation.2 | convolution fusion | flops 2416312320 | bytes 3407872 | tf_op jit(solution)/shard_map/dot_general | solution.py:168
  110.5 0.5 copy.43
  111.1 0.2 pad.5
  111.3 1.4 copy.39
  112.8 0.8 pad_maximum_fusion.s_ref
  113.8 69.6 %closure.1 = (f32[9,65536]{1,0:T(8,128)}, f32[320,256]{1,0:T(8,128)S(1)}) custom-call(bf16[16,65536]{1,0:T(8,128)(2,1)S(1)} %pad_maximum_fusion.s_ref, bf16[16,256]{1,0:T(8,128)(2,1)S(1)} %concatenate.14.w1_ref.wi_ref, f32[1,256]{1,0:T(1,128)S(1)} %bitcast.85, bf16[256,256]{1,0:T(8,128)(2,1)S(1)} %bitcast.83, bf16[256,256]{1,0:T(8,128)(2,1)S(1)} %copy-done.1, ...), custom_call_target="tpu_custom_call" | custom-call | tf_op jit(solution)/shard_map/closure/pallas_call | solution.py:228
  183.4 3.1 %copy.41 = f32[2,8,512,128]{3,2,1,0:T(8,128)S(1)} copy(f32[2,8,512,128]{3,1,2,0:T(8,128)} %bitcast.94) | data formatting | bytes 8388608
  186.6 1.6 slice.40
  188.1 24.6 %reduce_all.1 = f32[8,40,256]{2,1,0:T(8,128)} custom-call(f32[8,40,256]{2,1,0:T(8,128)} %bitcast.84), custom_call_target="tpu_custom_call" | custom-call | tf_op jit(solution)/shard_map/reduce_all/pallas_call | solution.py:318
  212.8 1.7 slice.37
  214.4 1.3 slice.35
  215.7 1.3 slice_bitcast_fusion
  217.0 1.3 fusion.4
  (53 shorter events, 2.2 us)
Async XLA Ops:
  0.6 5.3 %copy-start = (f32[3,1,16,32,128]{4,3,2,1,0:T(8,128)S(1)}, f32[3,1,16,32,128]{4,3,2,1,0:T(8,128)}, u32[]{:S(2)}) copy-start(f32[3,1,16,32,128]{4,3,2,1,0:T(8,128)} %param.17) | copy-start | bytes 2359300
  23.1 2.9 %copy-start.10 = (f32[176,256]{1,0:T(8,128)S(1)}, f32[176,256]{1,0:T(8,128)}, u32[]{:S(2)}) copy-start(f32[176,256]{1,0:T(8,128)} %constant.57.clone) | copy-start | bytes 540676
  51.0 2.8 %copy-start.11 = (f32[170,256]{1,0:T(8,128)S(1)}, f32[170,256]{1,0:T(8,128)}, u32[]{:S(2)}) copy-start(f32[170,256]{1,0:T(8,128)} %constant.58.clone) | copy-start | bytes 522244
  53.8 1.8 copy-start.14
  53.8 1.8 copy-start.5
  55.9 1.5 copy-start.8
  81.4 3.3 %copy-start.9 = (f32[256,176]{1,0:T(8,128)S(1)}, f32[256,176]{1,0:T(8,128)}, u32[]{:S(2)}) copy-start(f32[256,176]{1,0:T(8,128)} %constant.63.clone) | copy-start | bytes 540676
  105.7 2.1 copy-start.6
  107.8 3.3 %copy-start.7 = (bf16[9,1,16,32,128]{4,3,2,1,0:T(8,128)(2,1)S(1)}, bf16[9,1,16,32,128]{4,3,2,1,0:T(8,128)(2,1)}, u32[]{:S(2)}) copy-start(bf16[9,1,16,32,128]{4,3,2,1,0:T(8,128)(2,1)} %param.16) | copy-start | bytes 3538948
  112.8 0.9 copy-start.1
  112.8 1.0 copy-start.12
  112.8 1.0 copy-start.13
  112.8 1.1 copy-start.3
  112.8 1.1 copy-start.4
  183.4 3.1 %copy-start.2 = (f32[320,256]{1,0:T(8,128)}, f32[320,256]{1,0:T(8,128)S(1)}, u32[]{:S(2)}) copy-start(f32[320,256]{1,0:T(8,128)S(1)} %get-tuple-element.9) | copy-start | bytes 983044

commit v3 on v2

--- a/solution.py
+++ b/solution.py
@@ -133,16 +133,13 @@
     vel = [hat[:, :, comp] for comp in range(3)]
     inner = waves[0] * vel[0] + waves[1] * vel[1] + waves[2] * vel[2]
     square = jnp.maximum(waves[0] * waves[0] + waves[1] * waves[1] + waves[2] * waves[2], 1.0)
-    keep = (
-        (3 * jnp.abs(waves[0]) < nx) & (3 * jnp.abs(waves[1]) < ny) & (3 * jnp.abs(waves[2]) < nz)
-    )
-    proj = [jnp.where(keep, vel[i] - waves[i] * inner / square, 0.0) for i in range(3)]
+    proj = [vel[i] - waves[i] * inner / square for i in range(3)]
     sent = []
     for a, b in ((1, 1), (2, 2), (0, 1), (0, 2), (1, 2)):
         value = waves[a] * proj[a] if a == b else waves[b] * proj[a] + waves[a] * proj[b]
         sent.append((STEP_DT * value).reshape(2 * kx, ky, kz))
     ns = len(sent)
-    wide = 2 ** math.ceil(math.log2(ns * kz))
+    wide = 8 * (-(-(ns * kz) // 8))
     part = jnp.concatenate(sent + [jnp.zeros((2 * kx, ky, wide - ns * kz), jnp.float32)], axis=2)
     part = part.reshape(2 * kx, ky * wide)
     table = inverse_complex(mx, np.ones(kx), nx)
@@ -205,7 +202,8 @@
     delta_in = (back * (1.0 - wide * wide)).astype(jnp.bfloat16)
     acci[...] += jnp.dot(s, delta_in, preferred_element_type=jnp.float32)
     grad = lax.dot_general(wi_ref[...], delta_in, last, preferred_element_type=jnp.float32)
-    gx_ref[...] = grad[:feat]
+    for row in range(gx_ref.shape[1]):
+        gx_ref[:, row, :] = grad[:feat, row * 128 : (row + 1) * 128]
 
     @pl.when(step == steps - 1)
     def _():
@@ -239,11 +237,11 @@
             whole((ext, hid)),
         ],
         out_specs=[
-            pl.BlockSpec((feat, block), lambda i: (0, i)),
+            pl.BlockSpec((feat, block // 128, 128), lambda i: (0, i, 0)),
             whole((out_rows, hid)),
         ],
         out_shape=[
-            jax.ShapeDtypeStruct((feat, cells), jnp.float32),
+            jax.ShapeDtypeStruct((feat, cells // 128, 128), jnp.float32),
             jax.ShapeDtypeStruct((out_rows, hid), jnp.float32),
         ],
         scratch_shapes=[

time: 219 us -> 211 us (0.963)
  Pallas kernels: 155 us -> 151 us
  local copies, waits for them, and re-layouts: 48.3 us -> 45.4 us
    pallas_call x4, Pallas kernels: 60.3 us -> 56.5 us  [exchange(): pl.pallas_call(functools.partial(exchange_kernel, axis), out_shape=jax.Sh...]
    unnamed x36 -> x34, local copies, waits for them, and re-layouts: 7.08 us -> 3.48 us
    reshape x1 -> x2, local copies, waits for them, and re-layouts: 1.92 us -> 5.48 us  [spectral(): part = part.reshape(cols * 2, by, bx, wide).transpose(2, 1, 0, 3)]
    transpose x1 -> x0, local copies, waits for them, and re-layouts: 2.54 us -> none  [spectral(): part = part.reshape(cols * 2, by, bx, wide).transpose(2, 1, 0, 3)]
where the time goes in v3:
time: 211 us; the launch traced here: 210 us
  Pallas kernels  151 us (72%)
  local copies, waits for them, and re-layouts  45.4 us (22%)
  matrix products  10.2 us (5%)
  other arithmetic  2.57 us (1%)
    pallas_call x1, Pallas kernels, closure(): pl.pallas_call(functools.partial(closure_kernel, steps, feat), grid=(step...  69.8 us
    pallas_call x4, Pallas kernels, exchange(): pl.pallas_call(functools.partial(exchange_kernel, axis), out_shape=jax.Sh...  56.5 us
    pallas_call x1, Pallas kernels, reduce_all(): pl.pallas_call(functools.partial(reduce_kernel, rows, cols, factor), out_...  24.9 us
    reshape x2, local copies, waits for them, and re-layouts, spectral(): part = part.reshape(cols * 2, by, bx, wide).transpose(2, 1, 0, 3)  5.48 us

profile of v3, /device:TPU:25, one launch (start us, length us, event | category | flops | bytes accessed | tf_op | source)
XLA Modules:
  0.0 210.3 jit_solution(8550570114587208954)
XLA Ops:
  0.7 0.8 dynamic-slice_bitcast_fusion
  1.4 0.4 copy-done
  1.8 2.5 %fusion.6.x_ref = f32[4,22,1536]{2,1,0:T(8,128)} fusion(f32[4,22,128]{2,1,0:T(8,128)} %constant.62, f32[1536,128,1]{1,0,2:T(8,128)S(1)} %bitcast.76), kind=kOutput, calls=%fused_computation.23 | convolution fusion | flops 207618048 | bytes 1372160 | tf_op jit(solution)/shard_map/dot_general | solution.py:50
  4.3 10.3 %exchange_col.2 = f32[4,22,1536]{2,1,0:T(8,128)} custom-call(f32[4,22,1536]{2,1,0:T(8,128)} %fusion.6.x_ref), custom_call_target="tpu_custom_call" | custom-call | tf_op jit(solution)/shard_map/exchange_col/pallas_call | solution.py:92
  14.6 1.4 copy.26
  16.0 0.7 reshape.221
  16.7 2.2 %copy.27 = f32[11,3,16,2,4,32]{5,4,3,2,1,0:T(4,128)} copy(f32[11,3,16,2,4,32]{5,2,1,4,0,3:T(8,128)S(1)} %bitcast.82) | data formatting | bytes 1081344 | tf_op jit(solution)/shard_map/transpose | solution.py:116
  18.9 2.9 %reshape.222 = f32[528,256]{1,0:T(8,128)S(1)} reshape(f32[11,3,16,2,4,32]{5,4,3,2,1,0:T(4,128)} %copy.27) | data formatting | bytes 1081344 | tf_op jit(solution)/shard_map/reshape | solution.py:117
  21.8 0.8 fusion.7
  22.6 0.8 reshape.223.x_ref
  23.4 14.8 %exchange_row.2 = f32[8,22,528]{2,1,0:T(8,128)} custom-call(f32[8,22,528]{2,1,0:T(8,128)} %reshape.223.x_ref), custom_call_target="tpu_custom_call" | custom-call | tf_op jit(solution)/shard_map/exchange_row/pallas_call | solution.py:92
  38.2 1.1 copy.28
  39.4 3.5 %reshape.224 = f32[8,2,11,11,3,16]{5,4,3,0,2,1:T(4,128)} reshape(f32[8,22,528]{2,0,1:T(8,128)S(1)} %copy.28) | data formatting | bytes 743424 | tf_op jit(solution)/shard_map/reshape | solution.py:122
  42.9 4.0 %copy.29 = f32[3,11,11,2,8,16]{5,4,3,2,1,0:T(8,128)} copy(f32[3,11,11,2,8,16]{5,0,2,4,1,3:T(4,128)} %bitcast.81) | data formatting | bytes 743424 | tf_op jit(solution)/shard_map/transpose | solution.py:122
  46.9 2.8 %reshape.225 = f32[363,256]{1,0:T(8,128)S(1)} reshape(f32[3,11,11,2,8,16]{5,4,3,2,1,0:T(8,128)} %copy.29) | data formatting | bytes 743424 | tf_op jit(solution)/shard_map/reshape | solution.py:123
  49.7 0.5 fusion.8
  50.2 0.2 reshape.226
  50.5 0.2 fusion.4
  50.8 0.1 squeeze.21
  50.9 0.7 fusion.3
  51.7 0.7 fusion.2
  53.0 0.1 squeeze.19
  53.2 0.1 squeeze.20
  53.5 0.2 add_multiply_fusion
  53.7 0.1 add_multiply_fusion.1
  53.8 1.0 concatenate.12
  54.8 1.6 fusion.9
  56.5 17.9 %exchange_row.3 = f32[8,32,616]{2,1,0:T(8,128)} custom-call(f32[8,32,616]{2,1,0:T(8,128)} %bitcast.89), custom_call_target="tpu_custom_call" | custom-call | tf_op jit(solution)/shard_map/exchange_row/pallas_call | solution.py:92
  74.4 2.2 %reshape.229 = f32[16,16,11,56]{3,2,1,0:T(8,128)S(1)} reshape(f32[8,32,616]{2,1,0:T(8,128)} %exchange_row.3) | data formatting | bytes 1261568 | tf_op jit(solution)/shard_map/reshape | solution.py:150
  76.6 1.6 copy.34
  78.1 2.0 reshape.230
  80.1 1.9 fusion.10
  82.1 13.6 %exchange_col.3 = f32[4,64,896]{2,1,0:T(8,128)} custom-call(f32[4,64,896]{2,1,0:T(8,128)} %bitcast.88), custom_call_target="tpu_custom_call" | custom-call | tf_op jit(solution)/shard_map/exchange_col/pallas_call | solution.py:92
  95.6 2.9 %reshape.232 = f32[8,32,16,56]{3,2,1,0:T(8,128)S(1)} reshape(f32[4,64,896]{2,1,0:T(8,128)} %exchange_col.3) | data formatting | bytes 1835008 | tf_op jit(solution)/shard_map/reshape | solution.py:157
  98.6 2.5 %copy.46 = f32[8,32,16,56]{3,0,1,2:T(8,128)} copy(f32[8,32,16,56]{3,2,1,0:T(8,128)S(1)} %reshape.232) | data formatting | bytes 1835008 | tf_op jit(solution)/shard_map/reshape | solution.py:157
  101.1 2.1 %reshape.233 = f32[512,448]{1,0:T(8,128)S(1)} reshape(f32[16,32,8,56]{3,2,1,0:T(8,128)} %bitcast.85) | data formatting | bytes 1835008 | tf_op jit(solution)/shard_map/reshape | solution.py:158
  103.3 2.8 %fusion = bf16[1,6,512,128]{3,2,1,0:T(8,128)(2,1)S(1)} fusion(f32[6,128,448]{1,2,0:T(8,128)S(1)} %copy-done.5, f32[512,448]{1,0:T(8,128)S(1)} %reshape.233), kind=kOutput, calls=%fused_computation.3 | convolution fusion | flops 2114322432 | bytes 3080192 | tf_op jit(solution)/shard_map/dot_general | solution.py:165
  106.1 0.5 copy.47
  106.6 0.2 pad.5
  106.8 1.4 copy.42
  108.3 0.8 pad_maximum_fusion.s_ref
  109.4 69.8 %closure.1 = (f32[9,512,128]{2,1,0:T(8,128)}, f32[320,256]{1,0:T(8,128)S(1)}) custom-call(bf16[16,65536]{1,0:T(8,128)(2,1)S(1)} %pad_maximum_fusion.s_ref, bf16[16,256]{1,0:T(8,128)(2,1)S(1)} %concatenate.14.w1_ref.wi_ref, f32[1,256]{1,0:T(1,128)S(1)} %bitcast.79, bf16[256,256]{1,0:T(8,128)(2,1)S(1)} %bitcast.77, bf16[256,256]{1,0:T(8,128)(2,1)S(1)} %copy-done.1, ...), custom_call_target="tpu_custom_call" | custom-call | tf_op jit(solution)/shard_map/closure/pallas_call | solution.py:226
  179.2 0.7 copy-done.2
  179.9 24.9 %reduce_all.1 = f32[8,40,256]{2,1,0:T(8,128)} custom-call(f32[8,40,256]{2,1,0:T(8,128)} %bitcast.78), custom_call_target="tpu_custom_call" | custom-call | tf_op jit(solution)/shard_map/reduce_all/pallas_call | solution.py:316
  204.8 1.3 slice.35
  206.1 1.3 fusion.5
  207.4 1.7 slice.37
  209.0 1.3 slice_bitcast_fusion
  (45 shorter events, 1.4 us)
Async XLA Ops:
  0.6 1.2 copy-start
  18.9 2.9 %copy-start.9 = (f32[176,256]{1,0:T(8,128)S(1)}, f32[176,256]{1,0:T(8,128)}, u32[]{:S(2)}) copy-start(f32[176,256]{1,0:T(8,128)} %constant.50.clone) | copy-start | bytes 540676
  46.9 2.8 %copy-start.10 = (f32[170,256]{1,0:T(8,128)S(1)}, f32[170,256]{1,0:T(8,128)}, u32[]{:S(2)}) copy-start(f32[170,256]{1,0:T(8,128)} %constant.51.clone) | copy-start | bytes 522244
  49.7 2.9 %copy-start.13 = (f32[85]{0:T(128)S(1)}, f32[85]{0:T(128)}, u32[]{:S(2)}) copy-start(f32[85]{0:T(128)} %constant.63) | copy-start | bytes 1024
  49.7 3.7 %copy-start.14 = (f32[85]{0:T(128)S(1)}, f32[85]{0:T(128)}, u32[]{:S(2)}) copy-start(f32[85]{0:T(128)} %constant.52.clone) | copy-start | bytes 1024
  53.5 1.4 copy-start.8
  76.5 3.6 %copy-start.7 = (f32[256,176]{1,0:T(8,128)S(1)}, f32[256,176]{1,0:T(8,128)}, u32[]{:S(2)}) copy-start(f32[256,176]{1,0:T(8,128)} %constant.56.clone) | copy-start | bytes 540676
  101.1 2.1 %copy-start.5 = (f32[6,128,448]{1,2,0:T(8,128)S(1)}, f32[6,128,448]{1,2,0:T(8,128)}, u32[]{:S(2)}) copy-start(f32[6,128,448]{1,2,0:T(8,128)} %constant.65) | copy-start | bytes 4128772
  103.3 3.4 %copy-start.6 = (bf16[9,1,16,32,128]{4,3,2,1,0:T(8,128)(2,1)S(1)}, bf16[9,1,16,32,128]{4,3,2,1,0:T(8,128)(2,1)}, u32[]{:S(2)}) copy-start(bf16[9,1,16,32,128]{4,3,2,1,0:T(8,128)(2,1)} %param.16) | copy-start | bytes 3538948
  108.3 0.8 copy-start.11
  108.3 0.9 copy-start.1
  108.3 1.0 copy-start.12
  108.3 1.0 copy-start.3
  108.3 1.1 copy-start.4
  179.2 0.7 copy-start.2
